TPU v7x, 256 devices: a whole 4x4x8 slice. The times are simulated.
256 devices in a mesh: head: 16 (over x, y), qblk: 16 (over z, core).
Axes of the slice: x: 4, y: 4, z: 8, core: 2. Of those that a mesh axis runs over, the one named last changes fastest.
Arguments:
- queries: bfloat16 [32768, 4096], P(('qblk', 'head')), may hold values from -6 to 6
- key_states: bfloat16 [32768, 1024], P(('qblk', 'head')), may hold values from -6 to 6
- value_states: bfloat16 [32768, 1024], P(('qblk', 'head')), may hold values from -6 to 6
- vertical_blocks: int32 [32, 5], replicated, may hold values from 0 to 510, as said below
- slash_offsets: int32 [32, 8], replicated, may hold values from 1 to 64, as said below
Outputs:
- attended: bfloat16 [32768, 4096], P(('qblk', 'head'))
Inputs may be any that keep to these rules, and one draw needn't show every extreme that they name: `vertical_blocks`: each head names 5 distinct blocks, among them block 0 and block 510. `slash_offsets`: each head names 8 distinct offsets, among them 1 and 64.
All inputs are finite; a program needn't handle non-finite values.
Results may differ from a plain program's by a relative error of at most 0.0033.
Values may be sent and summed in bfloat16 or wider, within the bound.
No kernel may reach another device: no remote copies, remote signals or barrier semaphores. Data moves between devices by JAX's collectives and lax.ppermute only.
A program may use at most 64 MiB of HBM per device.

v0:
```python
import jax
import jax.numpy as jnp
from jax import lax
from jax.experimental import pallas as pl
from jax.experimental.pallas import tpu as pltpu
from jax.sharding import PartitionSpec as P


HD = 128
BLK = 64
NV = 5
NS = 8
NBD = 32
NSLOT = 8
LOG2E = 1.4426950408889634


SCALE = (HD**-0.5) * LOG2E
WROWS = 3 * 2048
G = 4
CH = 2


def attn_kernel(
    tab, qk2, vk2, own, swp, pk, pvk, vkv, o_ref, q_ref, ks, vs, bias, s0, s1, m0, m1, p0, p1, l0, l1, sem, sem1
):
    run = tab[0]
    odd = (run & 1) == 1
    copies = []
    for src, dst in (
        (qk2.at[:, pl.ds(0, 128)], q_ref.at[0]),
        (qk2.at[:, pl.ds(128, 128)], q_ref.at[1]),
        (qk2.at[:, pl.ds(256, BLK)], ks.at[pl.ds(0, 16), pl.ds(0, BLK)]),
        (vk2.at[:, pl.ds(128, BLK)], ks.at[pl.ds(0, 16), pl.ds(BLK, BLK)]),
        (vk2.at[:, pl.ds(0, 128)], vs.at[pl.ds(0, 16)]),
        (own.at[:, 0], ks.at[pl.ds(32, 16)]),
        (own.at[:, 1], vs.at[pl.ds(32, 16)]),
        (vkv.at[0], ks.at[pl.ds(48, NSLOT // 2)]),
        (vkv.at[1], vs.at[pl.ds(48, NSLOT // 2)]),
    ):
        copies.append(pltpu.make_async_copy(src, dst, sem.at[len(copies)]))
    for c in copies:
        c.start()

    def middle(pairs):
        return [pltpu.make_async_copy(src, dst, sem1.at[n]) for n, (src, dst) in enumerate(pairs)]

    lower = ks.at[pl.ds(16, 16), pl.ds(0, BLK)]
    upper = ks.at[pl.ds(16, 16), pl.ds(BLK, BLK)]
    values = vs.at[pl.ds(16, 16)]
    partner = middle(((pk, lower), (pvk.at[:, pl.ds(128, BLK)], upper), (pvk.at[:, pl.ds(0, 128)], values)))
    inner = middle(
        (
            (swp.at[:, 0, pl.ds(0, BLK)], lower),
            (swp.at[:, 0, pl.ds(BLK, BLK)], upper),
            (swp.at[:, 1], values),
        )
    )
    for cond, group in ((odd, inner), (jnp.logical_not(odd), partner)):

        @pl.when(cond)
        def _():
            for c in group:
                c.start()

    lane = lax.broadcasted_iota(jnp.int32, (8, 128), 1)
    slash = [[tab[19 + hh * NS + n] for n in range(NS)] for hh in range(2)]
    vert = [[tab[9 + hh * NV + n] for n in range(NV)] for hh in range(2)]
    spans = []
    for hh in range(2):
        named = [0] + slash[hh] + vert[hh]
        spans.append([jnp.where(lane < BLK, named[2 * c], named[2 * c + 1]) for c in range(7)])

    def mask(il, carry):
        for hh in range(2):
            for c in range(7):
                gap = run * NBD + il - spans[hh][c]
                bad = gap < 0
                if c >= 4:
                    hit = gap == 0
                    for s in slash[hh]:
                        hit = hit | (gap == s)
                    if c == 4:
                        hit = hit & (lane >= BLK)
                    bad = bad | hit
                bias[2 * il + hh, :, c * 128 : (c + 1) * 128] = jnp.where(bad, -jnp.inf, 0.0)
        return carry

    lax.fori_loop(0, NBD, mask, 0, unroll=4)
    for c in copies:
        c.wait()
    for c in partner:
        c.wait()

    rr = lax.broadcasted_iota(jnp.int32, (BLK, 128), 0)
    cc = lax.broadcasted_iota(jnp.int32, (BLK, 128), 1)
    causal = (rr >= cc) | (cc >= BLK)
    scores = (s0, s1)
    maxima = (m0, m1)
    probs = (p0, p1)
    totals = (l0, l1)
    queries = q_ref.reshape(2, NBD * BLK, HD)
    ksv = ks.reshape(52 * 128, HD)
    vsv = vs.reshape(52 * 128, HD)

    def rows_of(part, hh, il, n):
        if n <= NS:
            at = (2 * NBD + il) * BLK
            if n > 0:
                at = at - slash[hh][n - 1] * BLK
            return part[pl.ds(pl.multiple_of(at, BLK), BLK), :]
        slot = n - NS - 1 if hh == 0 else tab[35 + n - NS - 1]
        return part[pl.ds(pl.multiple_of(WROWS + slot * BLK, BLK), BLK), :]

    def first(t, buf):
        for g in range(G):
            il = t * (G // 2) + g // 2
            hh = g % 2
            row = pl.multiple_of(il * BLK, BLK)
            q = queries[hh, pl.ds(row, BLK), :]
            m = None
            for c0 in range(0, 7, CH):
                cs = list(range(c0, min(7, c0 + CH)))
                k = jnp.concatenate([rows_of(ksv, hh, il, 2 * c + j) for c in cs for j in range(2)], axis=0)
                xx = lax.dot_general(q, k, (((1,), (1,)), ((), ())), preferred_element_type=jnp.float32)
                for c in cs:
                    x = xx[:, (c - c0) * 128 : (c - c0 + 1) * 128]
                    x = x.reshape(8, 8, 128) + bias[2 * il + hh, :, c * 128 : (c + 1) * 128][None]
                    x = x.reshape(BLK, 128)
                    if c == 0:
                        x = jnp.where(causal, x, -jnp.inf)
                    scores[buf][g, :, c * 128 : (c + 1) * 128] = x
                    m = x if m is None else jnp.maximum(m, x)
            m = jnp.max(m, axis=1, keepdims=True)
            maxima[buf][g] = jnp.broadcast_to(m, (BLK, 128))

    def second(t, buf):
        for g in range(G):
            m = maxima[buf][g]
            total = None
            for c in range(7):
                p = jnp.exp2((scores[buf][g, :, c * 128 : (c + 1) * 128] - m) * SCALE)
                total = p if total is None else total + p
                probs[buf][g, :, c * 128 : (c + 1) * 128] = p.astype(jnp.bfloat16)
            total = jnp.sum(total, axis=1, keepdims=True)
            totals[buf][g] = jnp.broadcast_to(1.0 / total, (BLK, 128))

    def third(t, buf):
        for g in range(G):
            il = t * (G // 2) + g // 2
            hh = g % 2
            row = pl.multiple_of(il * BLK, BLK)
            v = jnp.concatenate([rows_of(vsv, hh, il, n) for n in range(14)], axis=0)
            acc = jnp.dot(probs[buf][g], v, preferred_element_type=jnp.float32)
            o_ref[pl.ds(row, BLK), hh * HD : (hh + 1) * HD] = (acc * totals[buf][g]).astype(o_ref.dtype)

    steps = 2 * NBD // G
    first(0, 0)
    first(1, 1)
    second(0, 0)

    def body(u, carry):
        t = 2 * u
        for e in range(2):
            third(t + e, e)
            first(jnp.minimum(t + e + 2, steps - 1), e)
            second(jnp.minimum(t + e + 1, steps - 1), 1 - e)
        return carry

    lax.fori_loop(0, steps // 2, body, 0)


def attend(tab, qk2, vk2, own, swp, pk, pvk, vkv):
    hbm = pl.BlockSpec(memory_space=pl.ANY)
    smem = pl.BlockSpec(memory_space=pltpu.SMEM)
    vmem = pl.BlockSpec(memory_space=pltpu.VMEM)
    return pl.pallas_call(
        attn_kernel,
        out_shape=jax.ShapeDtypeStruct((NBD * BLK, 2 * HD), jnp.bfloat16),
        in_specs=[smem] + [hbm] * 7,
        out_specs=vmem,
        scratch_shapes=[
            pltpu.VMEM((2, 16, 128, HD), jnp.bfloat16),
            pltpu.VMEM((52, 128, HD), jnp.bfloat16),
            pltpu.VMEM((52, 128, HD), jnp.bfloat16),
            pltpu.VMEM((2 * NBD, 8, 896), jnp.float32),
            pltpu.VMEM((G, BLK, 896), jnp.float32),
            pltpu.VMEM((G, BLK, 896), jnp.float32),
            pltpu.VMEM((G, BLK, 128), jnp.float32),
            pltpu.VMEM((G, BLK, 128), jnp.float32),
            pltpu.VMEM((G, BLK, 896), jnp.bfloat16),
            pltpu.VMEM((G, BLK, 896), jnp.bfloat16),
            pltpu.VMEM((G, BLK, 128), jnp.float32),
            pltpu.VMEM((G, BLK, 128), jnp.float32),
            pltpu.SemaphoreType.DMA((9,)),
            pltpu.SemaphoreType.DMA((3,)),
        ],
        cost_estimate=pl.CostEstimate(flops=2_000_000_000, bytes_accessed=6_000_000, transcendentals=4_000_000),
        name="attend",
    )(tab, qk2, vk2, own, swp, pk, pvk, vkv)


def pick_kernel(tab, kv, o_ref):
    run = tab[0]
    for n in range(NSLOT):
        local = tab[1 + n] - run * NBD
        at = jnp.clip(local, 0, NBD - 1)
        rows = pl.ds(pl.multiple_of((at & 1) * BLK, BLK), BLK)
        ok = jnp.full((BLK, HD), jnp.where(local == at, 1, 0), jnp.int32) == 1
        for part in range(2):
            x = kv[at >> 1, part, rows].astype(jnp.float32)
            dst = (part * NSLOT + n) * BLK
            o_ref[dst : dst + BLK, :] = jnp.where(ok, x, 0.0).astype(jnp.bfloat16)


def pick(tab, kv):
    vmem = pl.BlockSpec(memory_space=pltpu.VMEM)
    return pl.pallas_call(
        pick_kernel,
        out_shape=jax.ShapeDtypeStruct((NSLOT * 128, HD), jnp.bfloat16),
        in_specs=[pl.BlockSpec(memory_space=pltpu.SMEM), vmem],
        out_specs=vmem,
        cost_estimate=pl.CostEstimate(flops=1_000_000, bytes_accessed=1_500_000, transcendentals=0),
        name="pick",
    )(tab, kv)


def table(vertical_blocks, slash_offsets, head, run):
    vert = lax.dynamic_slice_in_dim(vertical_blocks, 2 * head, 2, 0)
    slash = lax.dynamic_slice_in_dim(slash_offsets, 2 * head, 2, 0)
    same = vert[1][:, None] == vert[0][None, :]
    fresh = jnp.logical_not(jnp.any(same, axis=1))
    n = jnp.arange(NV, dtype=jnp.int32)
    rank = jnp.sum(jnp.where((n[None, :] < n[:, None]) & fresh[None, :], 1, 0), axis=1)
    slot = jnp.where(fresh, NV + rank, jnp.sum(jnp.where(same, n[None, :], 0), axis=1))
    chosen = fresh[None, :] & (rank[None, :] == n[: NSLOT - NV, None])
    extra = jnp.sum(jnp.where(chosen, vert[1][None, :], 0), axis=1)
    parts = [run.reshape(1), vert[0], extra, vert.reshape(-1), slash.reshape(-1), slot]
    return jnp.concatenate([p.astype(jnp.int32) for p in parts])


def pack_kernel(q, k, o_ref):
    for d in range(16):
        for n in range(2):
            o_ref[d, n * 128 : n * 128 + 128] = q[:, (2 * d + n) * HD : (2 * d + n + 1) * HD]
        o_ref[d, 256 : 256 + BLK] = k[:, d // 2 * HD : (d // 2 + 1) * HD]


def pack(q, k):
    vmem = pl.BlockSpec(memory_space=pltpu.VMEM)
    return pl.pallas_call(
        pack_kernel,
        out_shape=jax.ShapeDtypeStruct((16, 256 + BLK, HD), jnp.bfloat16),
        in_specs=[vmem, vmem],
        out_specs=vmem,
        cost_estimate=pl.CostEstimate(flops=0, bytes_accessed=3_000_000, transcendentals=0),
        name="pack",
    )(q, k)


def pair_kernel(k, v, o_ref):
    for d in range(16):
        for n, x in enumerate((k, v)):
            o_ref[d, n] = x[:, d // 2 * HD : (d // 2 + 1) * HD]


def pair(k, v):
    vmem = pl.BlockSpec(memory_space=pltpu.VMEM)
    return pl.pallas_call(
        pair_kernel,
        out_shape=jax.ShapeDtypeStruct((16, 2, 128, HD), jnp.bfloat16),
        in_specs=[vmem, vmem],
        out_specs=vmem,
        cost_estimate=pl.CostEstimate(flops=0, bytes_accessed=2_000_000, transcendentals=0),
        name="pair",
    )(k, v)


def exchange(x, axis):
    return lax.all_to_all(x, axis, split_axis=0, concat_axis=0, tiled=True)


def per_device(queries, key_states, value_states, vertical_blocks, slash_offsets):
    runs = lax.axis_size("qblk")
    head = lax.axis_index("head")
    run = lax.axis_index("qblk").astype(jnp.int32)
    ahead = [(r, (r + 2) % runs) for r in range(runs)]
    swap = [(r, r ^ 1) for r in range(runs)]
    tab = table(vertical_blocks, slash_offsets, head, run)
    kv = pair(key_states, value_states)
    own = exchange(kv, "head")
    k2 = lax.ppermute(key_states[:BLK], "qblk", ahead)
    qk2 = pack(queries, k2)
    own, tab = lax.optimization_barrier((own, tab))
    cand = pick(tab, own).reshape(runs, NSLOT * 128 // runs, HD)
    cand = exchange(cand, "qblk")
    vk_own = jnp.concatenate([own[:, 1], own[:, 0, BLK:]], axis=1)
    vk2 = lax.ppermute(vk_own, "qblk", ahead)
    swp = lax.ppermute(own, "qblk", swap)
    pvk = lax.ppermute(vk2, "qblk", swap)
    part = jnp.sum(cand.astype(jnp.float32), axis=0).astype(jnp.bfloat16)
    vert = lax.all_gather(part, "qblk", axis=0, tiled=True)
    qk2 = exchange(qk2, "head")
    pk = lax.ppermute(qk2[:, 256:], "qblk", swap)
    out = attend(tab, qk2, vk2, own, swp, pk, pvk, vert.reshape(2, NSLOT // 2, 128, HD))
    return lax.all_to_all(out, "head", split_axis=0, concat_axis=1, tiled=True)


def solution(mesh):
    spec = P(("qblk", "head"), None)
    return jax.shard_map(
        per_device,
        mesh=mesh,
        in_specs=(spec, spec, spec, P(), P()),
        out_specs=spec,
        check_vma=False,
    )
```

profile of v0, /device:TPU:1, one launch (start us, length us, event | category | flops | bytes accessed | tf_op | source)
XLA Modules:
  0.0 129.2 jit_solution(12903649394651145622)
XLA Ops:
  0.0 2.1 %pair.1 = bf16[16,2,128,128]{3,2,1,0:T(8,128)(2,1)} custom-call(bf16[128,1024]{1,0:T(8,128)(2,1)} %k.1, bf16[128,1024]{1,0:T(8,128)(2,1)} %v.1), custom_call_target="tpu_custom_call" | custom-call | bytes 2000000 | tf_op jit(solution)/shard_map/pair/pallas_call | solution.py:269
  2.2 7.7 %all-to-all-start = ((bf16[16,2,128,128]{3,2,1,0:T(8,128)(2,1)}), bf16[16,2,128,128]{3,2,1,0:T(8,128)(2,1)S(1)}, u32[]{:S(2)}, u32[]{:S(2)}) async-start(bf16[16,2,128,128]{3,2,1,0:T(8,128)(2,1)} %pair.1), calls=%async_computation | async-start | bytes 2097152 | tf_op jit(solution)/shard_map/all_to_all | solution.py:280
  9.9 1.7 %collective-permute-start = (bf16[64,1024]{1,0:T(8,128)(2,1)S(1)}, bf16[64,1024]{1,0:T(8,128)(2,1)S(1)}, u32[]{:S(2)}, u32[]{:S(2)}) collective-permute-start(bf16[64,1024]{1,0:T(8,128)(2,1)S(1)} %slice.26), channel_id=1, source_target_pairs={{0,2},{1,3},{2,4},{3,5},{4,6},{5,7},{6,8},{7,9},{8,10},{9,11},{10,... | collective-permute-start | bytes 393224 | tf_op jit(solution)/shard_map/ppermute | solution.py:292
  11.9 0.2 compare_reduce_fusion
  12.7 0.2 select_reduce_fusion.1
  12.9 0.6 concatenate.6.tab
  13.4 5.0 %collective-permute-done.k = bf16[64,1024]{1,0:T(8,128)(2,1)S(1)} collective-permute-done((bf16[64,1024]{1,0:T(8,128)(2,1)S(1)}, bf16[64,1024]{1,0:T(8,128)(2,1)S(1)}, u32[]{:S(2)}, u32[]{:S(2)}) %collective-permute-start) | collective-permute-done | bytes 131104 | tf_op jit(solution)/shard_map/ppermute | solution.py:292
  18.5 0.6 copy-done.4
  19.1 2.5 %pack.1 = bf16[16,320,128]{2,1,0:T(8,128)(2,1)} custom-call(bf16[128,4096]{1,0:T(8,128)(2,1)} %q.1, bf16[64,1024]{1,0:T(8,128)(2,1)} %copy-done.4), custom_call_target="tpu_custom_call" | custom-call | bytes 3000000 | tf_op jit(solution)/shard_map/pack/pallas_call | solution.py:251
  21.6 3.9 %all-to-all-done.kv.own = bf16[16,2,128,128]{3,2,1,0:T(8,128)(2,1)S(1)} async-done(((bf16[16,2,128,128]{3,2,1,0:T(8,128)(2,1)}), bf16[16,2,128,128]{3,2,1,0:T(8,128)(2,1)S(1)}, u32[]{:S(2)}, u32[]{:S(2)}) %all-to-all-start) | async-done | bytes 1048608 | tf_op jit(solution)/shard_map/all_to_all | solution.py:280
  25.5 3.9 %all-to-all-start.1 = ((bf16[16,320,128]{2,1,0:T(8,128)(2,1)}), bf16[16,320,128]{2,1,0:T(8,128)(2,1)S(1)}, u32[]{:S(2)}, u32[]{:S(2)}) async-start(bf16[16,320,128]{2,1,0:T(8,128)(2,1)} %pack.1), calls=%async_computation.1 | async-start | bytes 2621440 | tf_op jit(solution)/shard_map/all_to_all | solution.py:280
  29.6 1.7 %collective-permute-start.1 = (bf16[16,192,128]{2,1,0:T(8,128)(2,1)S(1)}, bf16[16,192,128]{2,1,0:T(8,128)(2,1)}, u32[]{:S(2)}, u32[]{:S(2)}) collective-permute-start(bf16[16,192,128]{2,1,0:T(8,128)(2,1)S(1)} %pad_maximum_fusion), channel_id=1, source_target_pairs={{0,2},{1,3},{2,4},{3,5},{4,6},{5,7},{6,8},{7,9},{8,10},{9,11},{10,... | collective-permute-start | bytes 2359304 | tf_op jit(solution)/shard_map/ppermute | solution.py:298
  31.3 3.1 %collective-permute-start.2 = (bf16[16,2,128,128]{3,2,1,0:T(8,128)(2,1)S(1)}, bf16[16,2,128,128]{3,2,1,0:T(8,128)(2,1)}, u32[]{:S(2)}, u32[]{:S(2)}) collective-permute-start(bf16[16,2,128,128]{3,2,1,0:T(8,128)(2,1)S(1)} %all-to-all-done.kv.own), channel_id=1, source_target_pairs={{0,1},{1,0},{2,3},{3,2},{4,5},{5,4},{6,7},{7,6},{8,9},{9,8},{10,11... | collective-permute-start | bytes 3145736 | tf_op jit(solution)/shard_map/ppermute | solution.py:299
  34.4 16.0 %collective-permute-done.1.vk2 = bf16[16,192,128]{2,1,0:T(8,128)(2,1)} collective-permute-done((bf16[16,192,128]{2,1,0:T(8,128)(2,1)S(1)}, bf16[16,192,128]{2,1,0:T(8,128)(2,1)}, u32[]{:S(2)}, u32[]{:S(2)}) %collective-permute-start.1) | collective-permute-done | bytes 786464 | tf_op jit(solution)/shard_map/ppermute | solution.py:298
  50.4 3.4 %collective-permute-start.4 = (bf16[16,192,128]{2,1,0:T(8,128)(2,1)}, bf16[16,192,128]{2,1,0:T(8,128)(2,1)}, u32[]{:S(2)}, u32[]{:S(2)}) collective-permute-start(bf16[16,192,128]{2,1,0:T(8,128)(2,1)} %collective-permute-done.1.vk2), channel_id=1, source_target_pairs={{0,1},{1,0},{2,3},{3,2},{4,5},{5,4},{6,7},{7,6},{8,9},{9,8},{10,11... | collective-permute-start | bytes 2359304 | tf_op jit(solution)/shard_map/ppermute | solution.py:300
  53.8 2.0 %pick.1 = bf16[1024,128]{1,0:T(8,128)(2,1)} custom-call(s32[40]{0:T(128)} %concatenate.6.tab, bf16[16,2,128,128]{3,2,1,0:T(8,128)(2,1)} %copy-done.1), custom_call_target="tpu_custom_call" | custom-call | flops 1000000 | bytes 1500000 | tf_op jit(solution)/shard_map/pick/pallas_call | solution.py:218
  55.8 5.7 %all-to-all-start.2 = ((bf16[16,64,128]{2,1,0:T(8,128)(2,1)}), bf16[16,64,128]{2,1,0:T(8,128)(2,1)S(1)}, u32[]{:S(2)}, u32[]{:S(2)}) async-start(bf16[16,64,128]{2,1,0:T(8,128)(2,1)} %bitcast.13), calls=%async_computation.2 | async-start | bytes 524288 | tf_op jit(solution)/shard_map/all_to_all | solution.py:280
  61.5 0.2 collective-permute-start.3
  61.7 11.4 %all-to-all-done.2 = bf16[16,64,128]{2,1,0:T(8,128)(2,1)S(1)} async-done(((bf16[16,64,128]{2,1,0:T(8,128)(2,1)}), bf16[16,64,128]{2,1,0:T(8,128)(2,1)S(1)}, u32[]{:S(2)}, u32[]{:S(2)}) %all-to-all-start.2) | async-done | bytes 262176 | tf_op jit(solution)/shard_map/all_to_all | solution.py:280
  73.1 16.6 %all_gather.3 = bf16[1024,128]{1,0:T(8,128)(2,1)} all-gather(bf16[64,128]{1,0:T(8,128)(2,1)S(1)} %reduce_sum.42), channel_id=1, replica_groups=mesh['head'=16,'qblk'=16] {'qblk'}, dimensions={0}, use_global_device_ids=true | all-gather | bytes 278528 | tf_op jit(solution)/shard_map/all_gather | solution.py:302
  89.8 0.7 copy-done.6
  90.5 15.2 %attend.1 = bf16[2048,256]{1,0:T(8,128)(2,1)} custom-call(s32[40]{0:T(128)} %concatenate.6.tab, bf16[16,320,128]{2,1,0:T(8,128)(2,1)} %copy-done.2, bf16[16,192,128]{2,1,0:T(8,128)(2,1)} %collective-permute-done.1.vk2, bf16[16,2,128,128]{3,2,1,0:T(8,128)(2,1)} %copy-done.1, bf16[16,2,128,128]{3,2,1,0:T(8,128)(2,1)} %collective-permute-done.2.swp, ...), custom_call_target="tpu_custom_call" | custom-call | flops 2000000000 | bytes 6000000 | tf_op jit(solution)/shard_map/attend/pallas_call | solution.py:177
  105.7 22.5 %all_to_all.34 = bf16[16,128,256]{2,1,0:T(8,128)(2,1)S(1)} all-to-all(bf16[16,128,256]{2,1,0:T(8,128)(2,1)} %bitcast.14), channel_id=1, replica_groups=mesh['head'=16,'qblk'=16] {'head'}, dimensions={0} | all-to-all | bytes 2097152 | tf_op jit(solution)/shard_map/all_to_all | solution.py:306
  128.1 1.1 copy.23
  (33 shorter events, 1.1 us)
Async XLA Ops:
  0.0 12.3 %copy-start = (s32[32,8]{0,1:T(8,128)S(1)}, s32[32,8]{0,1:T(8,128)}, u32[]{:S(2)}) copy-start(s32[32,8]{0,1:T(8,128)} %param.9) | copy-start | bytes 3076
  2.1 7.7 %copy-start.3 = (bf16[128,1024]{1,0:T(8,128)(2,1)S(1)}, bf16[128,1024]{1,0:T(8,128)(2,1)}, u32[]{:S(2)}) copy-start(bf16[128,1024]{1,0:T(8,128)(2,1)} %k.1) | copy-start | bytes 786436
  2.2 9.5 %copy-start.5 = (s32[32,5]{0,1:T(8,128)S(1)}, s32[32,5]{0,1:T(8,128)}, u32[]{:S(2)}) copy-start(s32[32,5]{0,1:T(8,128)} %param.8) | copy-start | bytes 1924
  2.2 23.4 %all-to-all-start = ((bf16[16,2,128,128]{3,2,1,0:T(8,128)(2,1)}), bf16[16,2,128,128]{3,2,1,0:T(8,128)(2,1)S(1)}, u32[]{:S(2)}, u32[]{:S(2)}) async-start(bf16[16,2,128,128]{3,2,1,0:T(8,128)(2,1)} %pair.1), calls=%async_computation | async-start | bytes 2097152 | tf_op jit(solution)/shard_map/all_to_all | solution.py:280
  9.9 8.6 %collective-permute-start = (bf16[64,1024]{1,0:T(8,128)(2,1)S(1)}, bf16[64,1024]{1,0:T(8,128)(2,1)S(1)}, u32[]{:S(2)}, u32[]{:S(2)}) collective-permute-start(bf16[64,1024]{1,0:T(8,128)(2,1)S(1)} %slice.26), channel_id=1, source_target_pairs={{0,2},{1,3},{2,4},{3,5},{4,6},{5,7},{6,8},{7,9},{8,10},{9,11},{10,... | collective-permute-start | bytes 393224 | tf_op jit(solution)/shard_map/ppermute | solution.py:292
  18.5 0.6 copy-start.4
  25.5 5.8 %copy-start.1 = (bf16[16,2,128,128]{3,2,1,0:T(8,128)(2,1)}, bf16[16,2,128,128]{3,2,1,0:T(8,128)(2,1)S(1)}, u32[]{:S(2)}) copy-start(bf16[16,2,128,128]{3,2,1,0:T(8,128)(2,1)S(1)} %all-to-all-done.kv.own) | copy-start | bytes 3145732
  25.5 30.3 %all-to-all-start.1 = ((bf16[16,320,128]{2,1,0:T(8,128)(2,1)}), bf16[16,320,128]{2,1,0:T(8,128)(2,1)S(1)}, u32[]{:S(2)}, u32[]{:S(2)}) async-start(bf16[16,320,128]{2,1,0:T(8,128)(2,1)} %pack.1), calls=%async_computation.1 | async-start | bytes 2621440 | tf_op jit(solution)/shard_map/all_to_all | solution.py:280
  29.6 20.8 %collective-permute-start.1 = (bf16[16,192,128]{2,1,0:T(8,128)(2,1)S(1)}, bf16[16,192,128]{2,1,0:T(8,128)(2,1)}, u32[]{:S(2)}, u32[]{:S(2)}) collective-permute-start(bf16[16,192,128]{2,1,0:T(8,128)(2,1)S(1)} %pad_maximum_fusion), channel_id=1, source_target_pairs={{0,2},{1,3},{2,4},{3,5},{4,6},{5,7},{6,8},{7,9},{8,10},{9,11},{10,... | collective-permute-start | bytes 2359304 | tf_op jit(solution)/shard_map/ppermute | solution.py:298
  31.3 58.4 %collective-permute-start.2 = (bf16[16,2,128,128]{3,2,1,0:T(8,128)(2,1)S(1)}, bf16[16,2,128,128]{3,2,1,0:T(8,128)(2,1)}, u32[]{:S(2)}, u32[]{:S(2)}) collective-permute-start(bf16[16,2,128,128]{3,2,1,0:T(8,128)(2,1)S(1)} %all-to-all-done.kv.own), channel_id=1, source_target_pairs={{0,1},{1,0},{2,3},{3,2},{4,5},{5,4},{6,7},{7,6},{8,9},{9,8},{10,11... | collective-permute-start | bytes 3145736 | tf_op jit(solution)/shard_map/ppermute | solution.py:299
  50.4 39.3 %collective-permute-start.4 = (bf16[16,192,128]{2,1,0:T(8,128)(2,1)}, bf16[16,192,128]{2,1,0:T(8,128)(2,1)}, u32[]{:S(2)}, u32[]{:S(2)}) collective-permute-start(bf16[16,192,128]{2,1,0:T(8,128)(2,1)} %collective-permute-done.1.vk2), channel_id=1, source_target_pairs={{0,1},{1,0},{2,3},{3,2},{4,5},{5,4},{6,7},{7,6},{8,9},{9,8},{10,11... | collective-permute-start | bytes 2359304 | tf_op jit(solution)/shard_map/ppermute | solution.py:300
  55.8 33.9 %copy-start.2 = (bf16[16,320,128]{2,1,0:T(8,128)(2,1)}, bf16[16,320,128]{2,1,0:T(8,128)(2,1)S(1)}, u32[]{:S(2)}) copy-start(bf16[16,320,128]{2,1,0:T(8,128)(2,1)S(1)} %all-to-all-done.1.qk2) | copy-start | bytes 3932164
  55.8 17.3 %all-to-all-start.2 = ((bf16[16,64,128]{2,1,0:T(8,128)(2,1)}), bf16[16,64,128]{2,1,0:T(8,128)(2,1)S(1)}, u32[]{:S(2)}, u32[]{:S(2)}) async-start(bf16[16,64,128]{2,1,0:T(8,128)(2,1)} %bitcast.13), calls=%async_computation.2 | async-start | bytes 524288 | tf_op jit(solution)/shard_map/all_to_all | solution.py:280
  61.5 28.2 %collective-permute-start.3 = (bf16[16,64,128]{2,1,0:T(8,128)(2,1)S(1)}, bf16[16,64,128]{2,1,0:T(8,128)(2,1)S(1)}, u32[]{:S(2)}, u32[]{:S(2)}) collective-permute-start(bf16[16,64,128]{2,1,0:T(8,128)(2,1)S(1)} %slice.32), channel_id=1, source_target_pairs={{0,1},{1,0},{2,3},{3,2},{4,5},{5,4},{6,7},{7,6},{8,9},{9,8},{10,11... | collective-permute-start | bytes 786440 | tf_op jit(solution)/shard_map/ppermute | solution.py:304
  89.7 0.7 copy-start.6
where the time goes:
time: 130 us; the launch traced here: 129 us
  blocking collectives  39 us (30%)
  waiting for transfers between devices  36.3 us (28%)
  starting transfers between devices  27.5 us (21%)
  Pallas kernels  21.8 us (17%)
  local copies, waits for them, and re-layouts  3.76 us (3%)
    all_to_all x1, blocking collectives, per_device(): return lax.all_to_all(out, 'head', split_axis=0, concat_axis=1, tiled=True)  22.5 us
    all_to_all x3, starting transfers between devices, exchange(): return lax.all_to_all(x, axis, split_axis=0, concat_axis=0, tiled=True)  17.3 us
    all_gather x1, blocking collectives, per_device(): vert = lax.all_gather(part, 'qblk', axis=0, tiled=True)  16.6 us
    ppermute x1, waiting for transfers between devices, per_device(): vk2 = lax.ppermute(vk_own, 'qblk', ahead)  16 us
    all_to_all x3, waiting for transfers between devices, exchange(): return lax.all_to_all(x, axis, split_axis=0, concat_axis=0, tiled=True)  15.3 us
    pallas_call x1, Pallas kernels, attend(): pl.pallas_call(attn_kernel, out_shape=jax.ShapeDtypeStruct((NBD * BLK, 2...  15.2 us
    ppermute x1, waiting for transfers between devices, per_device(): k2 = lax.ppermute(key_states[:BLK], 'qblk', ahead)  5.02 us
    ppermute x1, starting transfers between devices, per_device(): pvk = lax.ppermute(vk2, 'qblk', swap)  3.43 us
  transfers between devices with their start and end apart: 8, of which 4 were waited for; matrix products, arithmetic and copies ran while one was open for 2% of the time, Pallas kernels for 3%

commit v1 on v0

--- a/solution.py
+++ b/solution.py
@@ -259,18 +259,19 @@
 
 
 def pair_kernel(k, v, o_ref):
-    for d in range(16):
+    for d in range(4):
         for n, x in enumerate((k, v)):
             o_ref[d, n] = x[:, d // 2 * HD : (d // 2 + 1) * HD]
 
 
 def pair(k, v):
-    vmem = pl.BlockSpec(memory_space=pltpu.VMEM)
+    tile = pl.BlockSpec((128, 2 * HD), lambda i: (0, i))
     return pl.pallas_call(
         pair_kernel,
+        grid=(4,),
         out_shape=jax.ShapeDtypeStruct((16, 2, 128, HD), jnp.bfloat16),
-        in_specs=[vmem, vmem],
-        out_specs=vmem,
+        in_specs=[tile, tile],
+        out_specs=pl.BlockSpec((4, 2, 128, HD), lambda i: (i, 0, 0, 0)),
         cost_estimate=pl.CostEstimate(flops=0, bytes_accessed=2_000_000, transcendentals=0),
         name="pair",
     )(k, v)

time: 130 us -> 131 us (level)
  no operation moved by 1% of the time
where the time goes in v1:
time: 131 us; the launch traced here: 130 us
  blocking collectives  39 us (30%)
  waiting for transfers between devices  36.3 us (28%)
  starting transfers between devices  27.5 us (21%)
  Pallas kernels  22.9 us (17%)
  local copies, waits for them, and re-layouts  3.76 us (3%)
    all_to_all x1, blocking collectives, per_device(): return lax.all_to_all(out, 'head', split_axis=0, concat_axis=1, tiled=True)  22.5 us
    all_to_all x3, starting transfers between devices, exchange(): return lax.all_to_all(x, axis, split_axis=0, concat_axis=0, tiled=True)  17.3 us
    all_gather x1, blocking collectives, per_device(): vert = lax.all_gather(part, 'qblk', axis=0, tiled=True)  16.6 us
    ppermute x1, waiting for transfers between devices, per_device(): vk2 = lax.ppermute(vk_own, 'qblk', ahead)  16 us
    all_to_all x3, waiting for transfers between devices, exchange(): return lax.all_to_all(x, axis, split_axis=0, concat_axis=0, tiled=True)  15.3 us
    pallas_call x1, Pallas kernels, attend(): pl.pallas_call(attn_kernel, out_shape=jax.ShapeDtypeStruct((NBD * BLK, 2...  15.2 us
    ppermute x1, waiting for transfers between devices, per_device(): k2 = lax.ppermute(key_states[:BLK], 'qblk', ahead)  5.02 us
    ppermute x1, starting transfers between devices, per_device(): pvk = lax.ppermute(vk2, 'qblk', swap)  3.43 us
  transfers between devices with their start and end apart: 8, of which 4 were waited for; matrix products, arithmetic and copies ran while one was open for 2% of the time, Pallas kernels for 3%

profile of v1, /device:TPU:1, one launch (start us, length us, event | category | flops | bytes accessed | tf_op | source)
XLA Modules:
  0.0 130.3 jit_solution(9273271636082786215)
XLA Ops:
  0.0 3.2 %pair.1 = bf16[16,2,128,128]{3,2,1,0:T(8,128)(2,1)} custom-call(bf16[128,1024]{1,0:T(8,128)(2,1)} %k.1, bf16[128,1024]{1,0:T(8,128)(2,1)} %v.1), custom_call_target="tpu_custom_call" | custom-call | bytes 2000000 | tf_op jit(solution)/shard_map/pair/pallas_call | solution.py:269
  3.3 7.7 %all-to-all-start = ((bf16[16,2,128,128]{3,2,1,0:T(8,128)(2,1)}), bf16[16,2,128,128]{3,2,1,0:T(8,128)(2,1)S(1)}, u32[]{:S(2)}, u32[]{:S(2)}) async-start(bf16[16,2,128,128]{3,2,1,0:T(8,128)(2,1)} %pair.1), calls=%async_computation | async-start | bytes 2097152 | tf_op jit(solution)/shard_map/all_to_all | solution.py:281
  11.0 1.7 %collective-permute-start = (bf16[64,1024]{1,0:T(8,128)(2,1)S(1)}, bf16[64,1024]{1,0:T(8,128)(2,1)S(1)}, u32[]{:S(2)}, u32[]{:S(2)}) collective-permute-start(bf16[64,1024]{1,0:T(8,128)(2,1)S(1)} %slice.26), channel_id=1, source_target_pairs={{0,2},{1,3},{2,4},{3,5},{4,6},{5,7},{6,8},{7,9},{8,10},{9,11},{10,... | collective-permute-start | bytes 393224 | tf_op jit(solution)/shard_map/ppermute | solution.py:293
  13.0 0.2 compare_reduce_fusion
  13.8 0.2 select_reduce_fusion.1
  14.0 0.6 concatenate.6.tab
  14.5 5.0 %collective-permute-done.k = bf16[64,1024]{1,0:T(8,128)(2,1)S(1)} collective-permute-done((bf16[64,1024]{1,0:T(8,128)(2,1)S(1)}, bf16[64,1024]{1,0:T(8,128)(2,1)S(1)}, u32[]{:S(2)}, u32[]{:S(2)}) %collective-permute-start) | collective-permute-done | bytes 131104 | tf_op jit(solution)/shard_map/ppermute | solution.py:293
  19.6 0.6 copy-done.4
  20.2 2.5 %pack.1 = bf16[16,320,128]{2,1,0:T(8,128)(2,1)} custom-call(bf16[128,4096]{1,0:T(8,128)(2,1)} %q.1, bf16[64,1024]{1,0:T(8,128)(2,1)} %copy-done.4), custom_call_target="tpu_custom_call" | custom-call | bytes 3000000 | tf_op jit(solution)/shard_map/pack/pallas_call | solution.py:251
  22.7 3.9 %all-to-all-done.kv.own = bf16[16,2,128,128]{3,2,1,0:T(8,128)(2,1)S(1)} async-done(((bf16[16,2,128,128]{3,2,1,0:T(8,128)(2,1)}), bf16[16,2,128,128]{3,2,1,0:T(8,128)(2,1)S(1)}, u32[]{:S(2)}, u32[]{:S(2)}) %all-to-all-start) | async-done | bytes 1048608 | tf_op jit(solution)/shard_map/all_to_all | solution.py:281
  26.6 3.9 %all-to-all-start.1 = ((bf16[16,320,128]{2,1,0:T(8,128)(2,1)}), bf16[16,320,128]{2,1,0:T(8,128)(2,1)S(1)}, u32[]{:S(2)}, u32[]{:S(2)}) async-start(bf16[16,320,128]{2,1,0:T(8,128)(2,1)} %pack.1), calls=%async_computation.1 | async-start | bytes 2621440 | tf_op jit(solution)/shard_map/all_to_all | solution.py:281
  30.7 1.7 %collective-permute-start.1 = (bf16[16,192,128]{2,1,0:T(8,128)(2,1)S(1)}, bf16[16,192,128]{2,1,0:T(8,128)(2,1)}, u32[]{:S(2)}, u32[]{:S(2)}) collective-permute-start(bf16[16,192,128]{2,1,0:T(8,128)(2,1)S(1)} %pad_maximum_fusion), channel_id=1, source_target_pairs={{0,2},{1,3},{2,4},{3,5},{4,6},{5,7},{6,8},{7,9},{8,10},{9,11},{10,... | collective-permute-start | bytes 2359304 | tf_op jit(solution)/shard_map/ppermute | solution.py:299
  32.4 3.1 %collective-permute-start.2 = (bf16[16,2,128,128]{3,2,1,0:T(8,128)(2,1)S(1)}, bf16[16,2,128,128]{3,2,1,0:T(8,128)(2,1)}, u32[]{:S(2)}, u32[]{:S(2)}) collective-permute-start(bf16[16,2,128,128]{3,2,1,0:T(8,128)(2,1)S(1)} %all-to-all-done.kv.own), channel_id=1, source_target_pairs={{0,1},{1,0},{2,3},{3,2},{4,5},{5,4},{6,7},{7,6},{8,9},{9,8},{10,11... | collective-permute-start | bytes 3145736 | tf_op jit(solution)/shard_map/ppermute | solution.py:300
  35.5 16.0 %collective-permute-done.1.vk2 = bf16[16,192,128]{2,1,0:T(8,128)(2,1)} collective-permute-done((bf16[16,192,128]{2,1,0:T(8,128)(2,1)S(1)}, bf16[16,192,128]{2,1,0:T(8,128)(2,1)}, u32[]{:S(2)}, u32[]{:S(2)}) %collective-permute-start.1) | collective-permute-done | bytes 786464 | tf_op jit(solution)/shard_map/ppermute | solution.py:299
  51.5 3.4 %collective-permute-start.4 = (bf16[16,192,128]{2,1,0:T(8,128)(2,1)}, bf16[16,192,128]{2,1,0:T(8,128)(2,1)}, u32[]{:S(2)}, u32[]{:S(2)}) collective-permute-start(bf16[16,192,128]{2,1,0:T(8,128)(2,1)} %collective-permute-done.1.vk2), channel_id=1, source_target_pairs={{0,1},{1,0},{2,3},{3,2},{4,5},{5,4},{6,7},{7,6},{8,9},{9,8},{10,11... | collective-permute-start | bytes 2359304 | tf_op jit(solution)/shard_map/ppermute | solution.py:301
  54.9 2.0 %pick.1 = bf16[1024,128]{1,0:T(8,128)(2,1)} custom-call(s32[40]{0:T(128)} %concatenate.6.tab, bf16[16,2,128,128]{3,2,1,0:T(8,128)(2,1)} %copy-done.1), custom_call_target="tpu_custom_call" | custom-call | flops 1000000 | bytes 1500000 | tf_op jit(solution)/shard_map/pick/pallas_call | solution.py:218
  56.9 5.7 %all-to-all-start.2 = ((bf16[16,64,128]{2,1,0:T(8,128)(2,1)}), bf16[16,64,128]{2,1,0:T(8,128)(2,1)S(1)}, u32[]{:S(2)}, u32[]{:S(2)}) async-start(bf16[16,64,128]{2,1,0:T(8,128)(2,1)} %bitcast.13), calls=%async_computation.2 | async-start | bytes 524288 | tf_op jit(solution)/shard_map/all_to_all | solution.py:281
  62.6 0.2 collective-permute-start.3
  62.8 11.4 %all-to-all-done.2 = bf16[16,64,128]{2,1,0:T(8,128)(2,1)S(1)} async-done(((bf16[16,64,128]{2,1,0:T(8,128)(2,1)}), bf16[16,64,128]{2,1,0:T(8,128)(2,1)S(1)}, u32[]{:S(2)}, u32[]{:S(2)}) %all-to-all-start.2) | async-done | bytes 262176 | tf_op jit(solution)/shard_map/all_to_all | solution.py:281
  74.2 16.6 %all_gather.3 = bf16[1024,128]{1,0:T(8,128)(2,1)} all-gather(bf16[64,128]{1,0:T(8,128)(2,1)S(1)} %reduce_sum.42), channel_id=1, replica_groups=mesh['head'=16,'qblk'=16] {'qblk'}, dimensions={0}, use_global_device_ids=true | all-gather | bytes 278528 | tf_op jit(solution)/shard_map/all_gather | solution.py:303
  90.9 0.7 copy-done.6
  91.5 15.2 %attend.1 = bf16[2048,256]{1,0:T(8,128)(2,1)} custom-call(s32[40]{0:T(128)} %concatenate.6.tab, bf16[16,320,128]{2,1,0:T(8,128)(2,1)} %copy-done.2, bf16[16,192,128]{2,1,0:T(8,128)(2,1)} %collective-permute-done.1.vk2, bf16[16,2,128,128]{3,2,1,0:T(8,128)(2,1)} %copy-done.1, bf16[16,2,128,128]{3,2,1,0:T(8,128)(2,1)} %collective-permute-done.2.swp, ...), custom_call_target="tpu_custom_call" | custom-call | flops 2000000000 | bytes 6000000 | tf_op jit(solution)/shard_map/attend/pallas_call | solution.py:177
  106.8 22.5 %all_to_all.34 = bf16[16,128,256]{2,1,0:T(8,128)(2,1)S(1)} all-to-all(bf16[16,128,256]{2,1,0:T(8,128)(2,1)} %bitcast.14), channel_id=1, replica_groups=mesh['head'=16,'qblk'=16] {'head'}, dimensions={0} | all-to-all | bytes 2097152 | tf_op jit(solution)/shard_map/all_to_all | solution.py:307
  129.2 1.1 copy.23
  (33 shorter events, 1.1 us)
Async XLA Ops:
  0.0 13.4 %copy-start = (s32[32,8]{0,1:T(8,128)S(1)}, s32[32,8]{0,1:T(8,128)}, u32[]{:S(2)}) copy-start(s32[32,8]{0,1:T(8,128)} %param.9) | copy-start | bytes 3076
  3.2 7.7 %copy-start.3 = (bf16[128,1024]{1,0:T(8,128)(2,1)S(1)}, bf16[128,1024]{1,0:T(8,128)(2,1)}, u32[]{:S(2)}) copy-start(bf16[128,1024]{1,0:T(8,128)(2,1)} %k.1) | copy-start | bytes 786436
  3.2 9.5 %copy-start.5 = (s32[32,5]{0,1:T(8,128)S(1)}, s32[32,5]{0,1:T(8,128)}, u32[]{:S(2)}) copy-start(s32[32,5]{0,1:T(8,128)} %param.8) | copy-start | bytes 1924
  3.3 23.4 %all-to-all-start = ((bf16[16,2,128,128]{3,2,1,0:T(8,128)(2,1)}), bf16[16,2,128,128]{3,2,1,0:T(8,128)(2,1)S(1)}, u32[]{:S(2)}, u32[]{:S(2)}) async-start(bf16[16,2,128,128]{3,2,1,0:T(8,128)(2,1)} %pair.1), calls=%async_computation | async-start | bytes 2097152 | tf_op jit(solution)/shard_map/all_to_all | solution.py:281
  11.0 8.6 %collective-permute-start = (bf16[64,1024]{1,0:T(8,128)(2,1)S(1)}, bf16[64,1024]{1,0:T(8,128)(2,1)S(1)}, u32[]{:S(2)}, u32[]{:S(2)}) collective-permute-start(bf16[64,1024]{1,0:T(8,128)(2,1)S(1)} %slice.26), channel_id=1, source_target_pairs={{0,2},{1,3},{2,4},{3,5},{4,6},{5,7},{6,8},{7,9},{8,10},{9,11},{10,... | collective-permute-start | bytes 393224 | tf_op jit(solution)/shard_map/ppermute | solution.py:293
  19.6 0.6 copy-start.4
  26.6 5.8 %copy-start.1 = (bf16[16,2,128,128]{3,2,1,0:T(8,128)(2,1)}, bf16[16,2,128,128]{3,2,1,0:T(8,128)(2,1)S(1)}, u32[]{:S(2)}) copy-start(bf16[16,2,128,128]{3,2,1,0:T(8,128)(2,1)S(1)} %all-to-all-done.kv.own) | copy-start | bytes 3145732
  26.6 30.3 %all-to-all-start.1 = ((bf16[16,320,128]{2,1,0:T(8,128)(2,1)}), bf16[16,320,128]{2,1,0:T(8,128)(2,1)S(1)}, u32[]{:S(2)}, u32[]{:S(2)}) async-start(bf16[16,320,128]{2,1,0:T(8,128)(2,1)} %pack.1), calls=%async_computation.1 | async-start | bytes 2621440 | tf_op jit(solution)/shard_map/all_to_all | solution.py:281
  30.7 20.8 %collective-permute-start.1 = (bf16[16,192,128]{2,1,0:T(8,128)(2,1)S(1)}, bf16[16,192,128]{2,1,0:T(8,128)(2,1)}, u32[]{:S(2)}, u32[]{:S(2)}) collective-permute-start(bf16[16,192,128]{2,1,0:T(8,128)(2,1)S(1)} %pad_maximum_fusion), channel_id=1, source_target_pairs={{0,2},{1,3},{2,4},{3,5},{4,6},{5,7},{6,8},{7,9},{8,10},{9,11},{10,... | collective-permute-start | bytes 2359304 | tf_op jit(solution)/shard_map/ppermute | solution.py:299
  32.4 58.4 %collective-permute-start.2 = (bf16[16,2,128,128]{3,2,1,0:T(8,128)(2,1)S(1)}, bf16[16,2,128,128]{3,2,1,0:T(8,128)(2,1)}, u32[]{:S(2)}, u32[]{:S(2)}) collective-permute-start(bf16[16,2,128,128]{3,2,1,0:T(8,128)(2,1)S(1)} %all-to-all-done.kv.own), channel_id=1, source_target_pairs={{0,1},{1,0},{2,3},{3,2},{4,5},{5,4},{6,7},{7,6},{8,9},{9,8},{10,11... | collective-permute-start | bytes 3145736 | tf_op jit(solution)/shard_map/ppermute | solution.py:300
  51.5 39.3 %collective-permute-start.4 = (bf16[16,192,128]{2,1,0:T(8,128)(2,1)}, bf16[16,192,128]{2,1,0:T(8,128)(2,1)}, u32[]{:S(2)}, u32[]{:S(2)}) collective-permute-start(bf16[16,192,128]{2,1,0:T(8,128)(2,1)} %collective-permute-done.1.vk2), channel_id=1, source_target_pairs={{0,1},{1,0},{2,3},{3,2},{4,5},{5,4},{6,7},{7,6},{8,9},{9,8},{10,11... | collective-permute-start | bytes 2359304 | tf_op jit(solution)/shard_map/ppermute | solution.py:301
  56.9 33.9 %copy-start.2 = (bf16[16,320,128]{2,1,0:T(8,128)(2,1)}, bf16[16,320,128]{2,1,0:T(8,128)(2,1)S(1)}, u32[]{:S(2)}) copy-start(bf16[16,320,128]{2,1,0:T(8,128)(2,1)S(1)} %all-to-all-done.1.qk2) | copy-start | bytes 3932164
  56.9 17.3 %all-to-all-start.2 = ((bf16[16,64,128]{2,1,0:T(8,128)(2,1)}), bf16[16,64,128]{2,1,0:T(8,128)(2,1)S(1)}, u32[]{:S(2)}, u32[]{:S(2)}) async-start(bf16[16,64,128]{2,1,0:T(8,128)(2,1)} %bitcast.13), calls=%async_computation.2 | async-start | bytes 524288 | tf_op jit(solution)/shard_map/all_to_all | solution.py:281
  62.6 28.2 %collective-permute-start.3 = (bf16[16,64,128]{2,1,0:T(8,128)(2,1)S(1)}, bf16[16,64,128]{2,1,0:T(8,128)(2,1)S(1)}, u32[]{:S(2)}, u32[]{:S(2)}) collective-permute-start(bf16[16,64,128]{2,1,0:T(8,128)(2,1)S(1)} %slice.32), channel_id=1, source_target_pairs={{0,1},{1,0},{2,3},{3,2},{4,5},{5,4},{6,7},{7,6},{8,9},{9,8},{10,11... | collective-permute-start | bytes 786440 | tf_op jit(solution)/shard_map/ppermute | solution.py:305
  90.8 0.7 copy-start.6

commit v2 on v0

--- a/solution.py
+++ b/solution.py
@@ -12,6 +12,7 @@
 NS = 8
 NBD = 32
 NSLOT = 8
+CUT = 96
 LOG2E = 1.4426950408889634
 
 
@@ -30,8 +31,8 @@
     for src, dst in (
         (qk2.at[:, pl.ds(0, 128)], q_ref.at[0]),
         (qk2.at[:, pl.ds(128, 128)], q_ref.at[1]),
-        (qk2.at[:, pl.ds(256, BLK)], ks.at[pl.ds(0, 16), pl.ds(0, BLK)]),
-        (vk2.at[:, pl.ds(128, BLK)], ks.at[pl.ds(0, 16), pl.ds(BLK, BLK)]),
+        (qk2.at[:, pl.ds(256, CUT)], ks.at[pl.ds(0, 16), pl.ds(0, CUT)]),
+        (vk2.at[:, pl.ds(128, 128 - CUT)], ks.at[pl.ds(0, 16), pl.ds(CUT, 128 - CUT)]),
         (vk2.at[:, pl.ds(0, 128)], vs.at[pl.ds(0, 16)]),
         (own.at[:, 0], ks.at[pl.ds(32, 16)]),
         (own.at[:, 1], vs.at[pl.ds(32, 16)]),
@@ -45,14 +46,14 @@
     def middle(pairs):
         return [pltpu.make_async_copy(src, dst, sem1.at[n]) for n, (src, dst) in enumerate(pairs)]
 
-    lower = ks.at[pl.ds(16, 16), pl.ds(0, BLK)]
-    upper = ks.at[pl.ds(16, 16), pl.ds(BLK, BLK)]
+    lower = ks.at[pl.ds(16, 16), pl.ds(0, CUT)]
+    upper = ks.at[pl.ds(16, 16), pl.ds(CUT, 128 - CUT)]
     values = vs.at[pl.ds(16, 16)]
-    partner = middle(((pk, lower), (pvk.at[:, pl.ds(128, BLK)], upper), (pvk.at[:, pl.ds(0, 128)], values)))
+    partner = middle(((pk, lower), (pvk.at[:, pl.ds(128, 128 - CUT)], upper), (pvk.at[:, pl.ds(0, 128)], values)))
     inner = middle(
         (
-            (swp.at[:, 0, pl.ds(0, BLK)], lower),
-            (swp.at[:, 0, pl.ds(BLK, BLK)], upper),
+            (swp.at[:, 0, pl.ds(0, CUT)], lower),
+            (swp.at[:, 0, pl.ds(CUT, 128 - CUT)], upper),
             (swp.at[:, 1], values),
         )
     )
@@ -243,14 +244,14 @@
     for d in range(16):
         for n in range(2):
             o_ref[d, n * 128 : n * 128 + 128] = q[:, (2 * d + n) * HD : (2 * d + n + 1) * HD]
-        o_ref[d, 256 : 256 + BLK] = k[:, d // 2 * HD : (d // 2 + 1) * HD]
+        o_ref[d, 256 : 256 + CUT] = k[:, d // 2 * HD : (d // 2 + 1) * HD]
 
 
 def pack(q, k):
     vmem = pl.BlockSpec(memory_space=pltpu.VMEM)
     return pl.pallas_call(
         pack_kernel,
-        out_shape=jax.ShapeDtypeStruct((16, 256 + BLK, HD), jnp.bfloat16),
+        out_shape=jax.ShapeDtypeStruct((16, 256 + CUT, HD), jnp.bfloat16),
         in_specs=[vmem, vmem],
         out_specs=vmem,
         cost_estimate=pl.CostEstimate(flops=0, bytes_accessed=3_000_000, transcendentals=0),
@@ -289,12 +290,12 @@
     tab = table(vertical_blocks, slash_offsets, head, run)
     kv = pair(key_states, value_states)
     own = exchange(kv, "head")
-    k2 = lax.ppermute(key_states[:BLK], "qblk", ahead)
+    k2 = lax.ppermute(key_states[:CUT], "qblk", ahead)
     qk2 = pack(queries, k2)
     own, tab = lax.optimization_barrier((own, tab))
     cand = pick(tab, own).reshape(runs, NSLOT * 128 // runs, HD)
     cand = exchange(cand, "qblk")
-    vk_own = jnp.concatenate([own[:, 1], own[:, 0, BLK:]], axis=1)
+    vk_own = jnp.concatenate([own[:, 1], own[:, 0, CUT:]], axis=1)
     vk2 = lax.ppermute(vk_own, "qblk", ahead)
     swp = lax.ppermute(own, "qblk", swap)
     pvk = lax.ppermute(vk2, "qblk", swap)

time: 130 us -> 127 us (0.977)
  waiting for transfers between devices: 36.3 us -> 34.3 us
    ppermute x1, waiting for transfers between devices: 16 us -> 13.2 us  [per_device(): vk2 = lax.ppermute(vk_own, 'qblk', ahead)]
    ppermute x1, waiting for transfers between devices: 5.02 us -> 7.42 us  [per_device(): k2 = lax.ppermute(key_states[:CUT], 'qblk', ahead)]
    all_to_all x3, waiting for transfers between devices: 15.3 us -> 13.7 us  [exchange(): return lax.all_to_all(x, axis, split_axis=0, concat_axis=0, tiled=True)]
  transfers between devices with their start and end apart: 8 -> 8, of which waited for: 4 -> 4; matrix products, arithmetic and copies ran while one was open for 2% -> 2% of each run, Pallas kernels for 3% -> 4%
where the time goes in v2:
time: 127 us
  blocking collectives  38.1 us (30%)
  waiting for transfers between devices  34.3 us (27%)
  starting transfers between devices  28.4 us (22%)
  Pallas kernels  21.9 us (17%)
  local copies, waits for them, and re-layouts  3.11 us (2%)
    all_to_all x1, blocking collectives, per_device(): return lax.all_to_all(out, 'head', split_axis=0, concat_axis=1, tiled=True)  21.6 us
    all_to_all x3, starting transfers between devices, exchange(): return lax.all_to_all(x, axis, split_axis=0, concat_axis=0, tiled=True)  18.3 us
    all_gather x1, blocking collectives, per_device(): vert = lax.all_gather(part, 'qblk', axis=0, tiled=True)  16.6 us
    pallas_call x1, Pallas kernels, attend(): pl.pallas_call(attn_kernel, out_shape=jax.ShapeDtypeStruct((NBD * BLK, 2...  15.2 us
    all_to_all x3, waiting for transfers between devices, exchange(): return lax.all_to_all(x, axis, split_axis=0, concat_axis=0, tiled=True)  13.7 us
    ppermute x1, waiting for transfers between devices, per_device(): vk2 = lax.ppermute(vk_own, 'qblk', ahead)  13.2 us
    ppermute x1, waiting for transfers between devices, per_device(): k2 = lax.ppermute(key_states[:CUT], 'qblk', ahead)  7.42 us
    ppermute x1, starting transfers between devices, per_device(): pvk = lax.ppermute(vk2, 'qblk', swap)  3.43 us
  transfers between devices with their start and end apart: 8, of which 4 were waited for; matrix products, arithmetic and copies ran while one was open for 2% of the time, Pallas kernels for 4%

profile of v2, /device:TPU:1, one launch (start us, length us, event | category | flops | bytes accessed | tf_op | source)
XLA Modules:
  0.0 126.7 jit_solution(5796129311298714212)
XLA Ops:
  0.0 2.1 %pair.1 = bf16[16,2,128,128]{3,2,1,0:T(8,128)(2,1)} custom-call(bf16[128,1024]{1,0:T(8,128)(2,1)} %k.1, bf16[128,1024]{1,0:T(8,128)(2,1)} %v.1), custom_call_target="tpu_custom_call" | custom-call | bytes 2000000 | tf_op jit(solution)/shard_map/pair/pallas_call | solution.py:270
  2.2 7.7 %all-to-all-start = ((bf16[16,2,128,128]{3,2,1,0:T(8,128)(2,1)}), bf16[16,2,128,128]{3,2,1,0:T(8,128)(2,1)S(1)}, u32[]{:S(2)}, u32[]{:S(2)}) async-start(bf16[16,2,128,128]{3,2,1,0:T(8,128)(2,1)} %pair.1), calls=%async_computation | async-start | bytes 2097152 | tf_op jit(solution)/shard_map/all_to_all | solution.py:281
  9.9 1.7 %collective-permute-start = (bf16[96,1024]{1,0:T(8,128)(2,1)S(1)}, bf16[96,1024]{1,0:T(8,128)(2,1)S(1)}, u32[]{:S(2)}, u32[]{:S(2)}) collective-permute-start(bf16[96,1024]{1,0:T(8,128)(2,1)S(1)} %slice.26), channel_id=1, source_target_pairs={{0,2},{1,3},{2,4},{3,5},{4,6},{5,7},{6,8},{7,9},{8,10},{9,11},{10,... | collective-permute-start | bytes 589832 | tf_op jit(solution)/shard_map/ppermute | solution.py:293
  11.7 0.2 slice_reduce_fusion
  11.9 0.2 compare_reduce_fusion
  12.3 0.2 select_reduce_fusion.1
  12.5 7.4 %collective-permute-done.k = bf16[96,1024]{1,0:T(8,128)(2,1)S(1)} collective-permute-done((bf16[96,1024]{1,0:T(8,128)(2,1)S(1)}, bf16[96,1024]{1,0:T(8,128)(2,1)S(1)}, u32[]{:S(2)}, u32[]{:S(2)}) %collective-permute-start) | collective-permute-done | bytes 196640 | tf_op jit(solution)/shard_map/ppermute | solution.py:293
  19.9 0.7 copy-done.4
  20.6 2.6 %pack.1 = bf16[16,352,128]{2,1,0:T(8,128)(2,1)} custom-call(bf16[128,4096]{1,0:T(8,128)(2,1)} %q.1, bf16[96,1024]{1,0:T(8,128)(2,1)} %copy-done.4), custom_call_target="tpu_custom_call" | custom-call | bytes 3000000 | tf_op jit(solution)/shard_map/pack/pallas_call | solution.py:252
  23.2 2.4 %all-to-all-done.kv.own = bf16[16,2,128,128]{3,2,1,0:T(8,128)(2,1)S(1)} async-done(((bf16[16,2,128,128]{3,2,1,0:T(8,128)(2,1)}), bf16[16,2,128,128]{3,2,1,0:T(8,128)(2,1)S(1)}, u32[]{:S(2)}, u32[]{:S(2)}) %all-to-all-start) | async-done | bytes 1048608 | tf_op jit(solution)/shard_map/all_to_all | solution.py:281
  25.5 4.0 %all-to-all-start.1 = ((bf16[16,352,128]{2,1,0:T(8,128)(2,1)}), bf16[16,352,128]{2,1,0:T(8,128)(2,1)S(1)}, u32[]{:S(2)}, u32[]{:S(2)}) async-start(bf16[16,352,128]{2,1,0:T(8,128)(2,1)} %pack.1), calls=%async_computation.1 | async-start | bytes 2883584 | tf_op jit(solution)/shard_map/all_to_all | solution.py:281
  30.0 0.6 concatenate.6.tab
  30.6 1.6 %collective-permute-start.1 = (bf16[16,160,128]{2,1,0:T(8,128)(2,1)S(1)}, bf16[16,160,128]{2,1,0:T(8,128)(2,1)}, u32[]{:S(2)}, u32[]{:S(2)}) collective-permute-start(bf16[16,160,128]{2,1,0:T(8,128)(2,1)S(1)} %pad_maximum_fusion), channel_id=1, source_target_pairs={{0,2},{1,3},{2,4},{3,5},{4,6},{5,7},{6,8},{7,9},{8,10},{9,11},{10,... | collective-permute-start | bytes 1966088 | tf_op jit(solution)/shard_map/ppermute | solution.py:299
  32.3 3.1 %collective-permute-start.2 = (bf16[16,2,128,128]{3,2,1,0:T(8,128)(2,1)S(1)}, bf16[16,2,128,128]{3,2,1,0:T(8,128)(2,1)}, u32[]{:S(2)}, u32[]{:S(2)}) collective-permute-start(bf16[16,2,128,128]{3,2,1,0:T(8,128)(2,1)S(1)} %all-to-all-done.kv.own), channel_id=1, source_target_pairs={{0,1},{1,0},{2,3},{3,2},{4,5},{5,4},{6,7},{7,6},{8,9},{9,8},{10,11... | collective-permute-start | bytes 3145736 | tf_op jit(solution)/shard_map/ppermute | solution.py:300
  35.4 13.2 %collective-permute-done.1.vk2 = bf16[16,160,128]{2,1,0:T(8,128)(2,1)} collective-permute-done((bf16[16,160,128]{2,1,0:T(8,128)(2,1)S(1)}, bf16[16,160,128]{2,1,0:T(8,128)(2,1)}, u32[]{:S(2)}, u32[]{:S(2)}) %collective-permute-start.1) | collective-permute-done | bytes 655392 | tf_op jit(solution)/shard_map/ppermute | solution.py:299
  48.6 3.4 %collective-permute-start.4 = (bf16[16,160,128]{2,1,0:T(8,128)(2,1)}, bf16[16,160,128]{2,1,0:T(8,128)(2,1)}, u32[]{:S(2)}, u32[]{:S(2)}) collective-permute-start(bf16[16,160,128]{2,1,0:T(8,128)(2,1)} %collective-permute-done.1.vk2), channel_id=1, source_target_pairs={{0,1},{1,0},{2,3},{3,2},{4,5},{5,4},{6,7},{7,6},{8,9},{9,8},{10,11... | collective-permute-start | bytes 1966088 | tf_op jit(solution)/shard_map/ppermute | solution.py:301
  52.0 2.0 %pick.1 = bf16[1024,128]{1,0:T(8,128)(2,1)} custom-call(s32[40]{0:T(128)} %concatenate.6.tab, bf16[16,2,128,128]{3,2,1,0:T(8,128)(2,1)} %copy-done.1), custom_call_target="tpu_custom_call" | custom-call | flops 1000000 | bytes 1500000 | tf_op jit(solution)/shard_map/pick/pallas_call | solution.py:219
  54.0 6.6 %all-to-all-start.2 = ((bf16[16,64,128]{2,1,0:T(8,128)(2,1)}), bf16[16,64,128]{2,1,0:T(8,128)(2,1)S(1)}, u32[]{:S(2)}, u32[]{:S(2)}) async-start(bf16[16,64,128]{2,1,0:T(8,128)(2,1)} %bitcast.13), calls=%async_computation.2 | async-start | bytes 524288 | tf_op jit(solution)/shard_map/all_to_all | solution.py:281
  60.6 0.2 collective-permute-start.3
  60.8 11.4 %all-to-all-done.2 = bf16[16,64,128]{2,1,0:T(8,128)(2,1)S(1)} async-done(((bf16[16,64,128]{2,1,0:T(8,128)(2,1)}), bf16[16,64,128]{2,1,0:T(8,128)(2,1)S(1)}, u32[]{:S(2)}, u32[]{:S(2)}) %all-to-all-start.2) | async-done | bytes 262176 | tf_op jit(solution)/shard_map/all_to_all | solution.py:281
  72.2 16.6 %all_gather.3 = bf16[1024,128]{1,0:T(8,128)(2,1)} all-gather(bf16[64,128]{1,0:T(8,128)(2,1)S(1)} %reduce_sum.42), channel_id=1, replica_groups=mesh['head'=16,'qblk'=16] {'qblk'}, dimensions={0}, use_global_device_ids=true | all-gather | bytes 278528 | tf_op jit(solution)/shard_map/all_gather | solution.py:303
  88.8 15.2 %attend.1 = bf16[2048,256]{1,0:T(8,128)(2,1)} custom-call(s32[40]{0:T(128)} %concatenate.6.tab, bf16[16,352,128]{2,1,0:T(8,128)(2,1)} %copy-done.2, bf16[16,160,128]{2,1,0:T(8,128)(2,1)} %collective-permute-done.1.vk2, bf16[16,2,128,128]{3,2,1,0:T(8,128)(2,1)} %copy-done.1, bf16[16,2,128,128]{3,2,1,0:T(8,128)(2,1)} %collective-permute-done.2.swp, ...), custom_call_target="tpu_custom_call" | custom-call | flops 2000000000 | bytes 6000000 | tf_op jit(solution)/shard_map/attend/pallas_call | solution.py:178
  104.0 21.6 %all_to_all.34 = bf16[16,128,256]{2,1,0:T(8,128)(2,1)S(1)} all-to-all(bf16[16,128,256]{2,1,0:T(8,128)(2,1)} %bitcast.14), channel_id=1, replica_groups=mesh['head'=16,'qblk'=16] {'head'}, dimensions={0} | all-to-all | bytes 2097152 | tf_op jit(solution)/shard_map/all_to_all | solution.py:307
  125.6 1.1 copy.23
  (31 shorter events, 0.9 us)
Async XLA Ops:
  0.0 29.5 %copy-start = (s32[32,8]{0,1:T(8,128)S(1)}, s32[32,8]{0,1:T(8,128)}, u32[]{:S(2)}) copy-start(s32[32,8]{0,1:T(8,128)} %param.9) | copy-start | bytes 3076
  2.1 7.7 %copy-start.3 = (bf16[128,1024]{1,0:T(8,128)(2,1)S(1)}, bf16[128,1024]{1,0:T(8,128)(2,1)}, u32[]{:S(2)}) copy-start(bf16[128,1024]{1,0:T(8,128)(2,1)} %k.1) | copy-start | bytes 786436
  2.2 9.5 %copy-start.5 = (s32[32,5]{0,1:T(8,128)S(1)}, s32[32,5]{0,1:T(8,128)}, u32[]{:S(2)}) copy-start(s32[32,5]{0,1:T(8,128)} %param.8) | copy-start | bytes 1924
  2.2 23.4 %all-to-all-start = ((bf16[16,2,128,128]{3,2,1,0:T(8,128)(2,1)}), bf16[16,2,128,128]{3,2,1,0:T(8,128)(2,1)S(1)}, u32[]{:S(2)}, u32[]{:S(2)}) async-start(bf16[16,2,128,128]{3,2,1,0:T(8,128)(2,1)} %pair.1), calls=%async_computation | async-start | bytes 2097152 | tf_op jit(solution)/shard_map/all_to_all | solution.py:281
  9.9 10.0 %collective-permute-start = (bf16[96,1024]{1,0:T(8,128)(2,1)S(1)}, bf16[96,1024]{1,0:T(8,128)(2,1)S(1)}, u32[]{:S(2)}, u32[]{:S(2)}) collective-permute-start(bf16[96,1024]{1,0:T(8,128)(2,1)S(1)} %slice.26), channel_id=1, source_target_pairs={{0,2},{1,3},{2,4},{3,5},{4,6},{5,7},{6,8},{7,9},{8,10},{9,11},{10,... | collective-permute-start | bytes 589832 | tf_op jit(solution)/shard_map/ppermute | solution.py:293
  19.9 0.7 copy-start.4
  25.5 6.7 %copy-start.1 = (bf16[16,2,128,128]{3,2,1,0:T(8,128)(2,1)}, bf16[16,2,128,128]{3,2,1,0:T(8,128)(2,1)S(1)}, u32[]{:S(2)}) copy-start(bf16[16,2,128,128]{3,2,1,0:T(8,128)(2,1)S(1)} %all-to-all-done.kv.own) | copy-start | bytes 3145732
  25.5 28.5 %all-to-all-start.1 = ((bf16[16,352,128]{2,1,0:T(8,128)(2,1)}), bf16[16,352,128]{2,1,0:T(8,128)(2,1)S(1)}, u32[]{:S(2)}, u32[]{:S(2)}) async-start(bf16[16,352,128]{2,1,0:T(8,128)(2,1)} %pack.1), calls=%async_computation.1 | async-start | bytes 2883584 | tf_op jit(solution)/shard_map/all_to_all | solution.py:281
  30.6 17.9 %collective-permute-start.1 = (bf16[16,160,128]{2,1,0:T(8,128)(2,1)S(1)}, bf16[16,160,128]{2,1,0:T(8,128)(2,1)}, u32[]{:S(2)}, u32[]{:S(2)}) collective-permute-start(bf16[16,160,128]{2,1,0:T(8,128)(2,1)S(1)} %pad_maximum_fusion), channel_id=1, source_target_pairs={{0,2},{1,3},{2,4},{3,5},{4,6},{5,7},{6,8},{7,9},{8,10},{9,11},{10,... | collective-permute-start | bytes 1966088 | tf_op jit(solution)/shard_map/ppermute | solution.py:299
  32.3 56.5 %collective-permute-start.2 = (bf16[16,2,128,128]{3,2,1,0:T(8,128)(2,1)S(1)}, bf16[16,2,128,128]{3,2,1,0:T(8,128)(2,1)}, u32[]{:S(2)}, u32[]{:S(2)}) collective-permute-start(bf16[16,2,128,128]{3,2,1,0:T(8,128)(2,1)S(1)} %all-to-all-done.kv.own), channel_id=1, source_target_pairs={{0,1},{1,0},{2,3},{3,2},{4,5},{5,4},{6,7},{7,6},{8,9},{9,8},{10,11... | collective-permute-start | bytes 3145736 | tf_op jit(solution)/shard_map/ppermute | solution.py:300
  48.6 40.2 %collective-permute-start.4 = (bf16[16,160,128]{2,1,0:T(8,128)(2,1)}, bf16[16,160,128]{2,1,0:T(8,128)(2,1)}, u32[]{:S(2)}, u32[]{:S(2)}) collective-permute-start(bf16[16,160,128]{2,1,0:T(8,128)(2,1)} %collective-permute-done.1.vk2), channel_id=1, source_target_pairs={{0,1},{1,0},{2,3},{3,2},{4,5},{5,4},{6,7},{7,6},{8,9},{9,8},{10,11... | collective-permute-start | bytes 1966088 | tf_op jit(solution)/shard_map/ppermute | solution.py:301
  54.0 34.8 %copy-start.2 = (bf16[16,352,128]{2,1,0:T(8,128)(2,1)}, bf16[16,352,128]{2,1,0:T(8,128)(2,1)S(1)}, u32[]{:S(2)}) copy-start(bf16[16,352,128]{2,1,0:T(8,128)(2,1)S(1)} %all-to-all-done.1.qk2) | copy-start | bytes 4325380
  54.0 18.2 %all-to-all-start.2 = ((bf16[16,64,128]{2,1,0:T(8,128)(2,1)}), bf16[16,64,128]{2,1,0:T(8,128)(2,1)S(1)}, u32[]{:S(2)}, u32[]{:S(2)}) async-start(bf16[16,64,128]{2,1,0:T(8,128)(2,1)} %bitcast.13), calls=%async_computation.2 | async-start | bytes 524288 | tf_op jit(solution)/shard_map/all_to_all | solution.py:281
  60.6 28.2 %collective-permute-start.3 = (bf16[16,96,128]{2,1,0:T(8,128)(2,1)S(1)}, bf16[16,96,128]{2,1,0:T(8,128)(2,1)}, u32[]{:S(2)}, u32[]{:S(2)}) collective-permute-start(bf16[16,96,128]{2,1,0:T(8,128)(2,1)S(1)} %slice.32), channel_id=1, source_target_pairs={{0,1},{1,0},{2,3},{3,2},{4,5},{5,4},{6,7},{7,6},{8,9},{9,8},{10,11... | collective-permute-start | bytes 1179656 | tf_op jit(solution)/shard_map/ppermute | solution.py:305
